TPU v7x, 256 devices: a whole 4x4x8 slice. The times are simulated.
256 devices in a mesh: cfg: 2 (over core), req: 8 (over z), seq: 16 (over y, x).
Axes of the slice: x: 4, y: 4, z: 8, core: 2. Of those that a mesh axis runs over, the one named last changes fastest.
Arguments:
- queries: bfloat16 [2, 8, 768, 1536], P('cfg', 'req', 'seq'), may hold values from -50 to 50
- text_cache: bfloat16 [2, 8, 2, 512, 1536], P('cfg', 'req'), may hold values from -6 to 6
- image_cache: bfloat16 [2, 8, 2, 768, 1536], P('cfg', 'req'), may hold values from -6 to 6
- fresh_kv: bfloat16 [2, 8, 2, 96, 1536], P('cfg', 'req', None, 'seq'), may hold values from -6 to 6
- fresh_slots: int32 [8, 96], P('req'), may hold values from 0 to 767, as said below
- fresh_pos: int32 [3, 8, 96], P(None, 'req', 'seq'), may hold values from 0 to 63
- image_len: int32 [8], replicated, may hold values from 384 to 768, as said below
- stream: bfloat16 [2, 8, 768, 3072], P('cfg', None, 'seq', 'req'), may hold values from -30 to 30
- modulation: float32 [2, 8, 4, 3072], replicated, may hold values from -4 to 4
- out_weight: bfloat16 [1536, 3072], P('seq', 'req'), may hold values from -0.15625 to 0.15625
- up_weight: bfloat16 [3072, 12288], P('seq', 'req'), may hold values from -0.109375 to 0.109375
- down_weight: bfloat16 [12288, 3072], P('req', 'seq'), may hold values from -0.0546875 to 0.0546875
- final_weight: bfloat16 [3072, 64], replicated, may hold values from -0.109375 to 0.109375
- latent: float32 [8, 384, 128], P('req', 'seq', 'cfg'), may hold values from -6 to 6
- step_index: int32 [1], replicated, may hold values from 0 to 27
Outputs:
- latent_next: float32 [8, 384, 128], P('req', 'seq', 'cfg')
- denoised: float32 [8, 384, 128], P('req', 'seq', 'cfg')
Inputs may be any that keep to these rules, and one draw needn't show every extreme that they name: `fresh_slots`: columns k * 6 to (k + 1) * 6 - 1 of a row hold distinct slots from k * 48 to (k + 1) * 48 - 1. `image_len`: some request has exactly 768 image tokens and some other exactly 384.
All inputs are finite; a program needn't handle non-finite values.
Results may differ from a plain program's by a relative error of at most 0.0095.
Values may be sent and summed in bfloat16 or wider, within the bound.
A program may use at most 128 MiB of HBM per device.

v0:
```python
import math
import jax
import jax.numpy as jnp
from jax import lax
from jax.sharding import PartitionSpec as P

STEPS = 28
GUIDANCE = 3.0
SHIFT = 3.0
SCALE = 1.0 / math.sqrt(128.0)
EPSILON = 1e-06


def swapped(block, axis, stride):
    count = lax.axis_size(axis)
    route = []
    for low in range(count):
        high = low | 1 << stride
        if high != low and high < count:
            route += [(low, high), (high, low)]
    return lax.ppermute(block, axis, route)


def rope_angles(positions):
    columns = []
    for component, axis_span in ((0, 16), (1, 56), (2, 56)):
        pair_ids = jnp.arange(axis_span // 2, dtype=jnp.float32)
        frequency = jnp.exp(-(2.0 * pair_ids / axis_span) * math.log(10000.0))
        columns.append(positions[component].astype(jnp.float32)[:, None] * frequency[None, :])
    return jnp.concatenate(columns, axis=1)


def rotate(key_rows, angles):
    row_total = key_rows.shape[0]
    paired = key_rows.reshape(row_total, -1, 64, 2)
    cosine = jnp.cos(angles)[:, None, :]
    sine = jnp.sin(angles)[:, None, :]
    first = cosine * paired[..., 0] - sine * paired[..., 1]
    second = sine * paired[..., 0] + cosine * paired[..., 1]
    return jnp.stack([first, second], axis=-1).reshape(row_total, -1)


def noise_level(index):
    fraction = 1.0 - index.astype(jnp.float32) / STEPS
    return SHIFT * fraction / (SHIFT * fraction + 1.0 - fraction)


def head_scores(query_heads, key_rows):
    key_heads = key_rows.reshape(key_rows.shape[0], -1, 128)
    return (
        jnp.einsum("qhd,khd->hqk", query_heads, key_heads, preferred_element_type=jnp.float32)
        * SCALE
    )


def head_mix(weights, value_rows):
    value_heads = value_rows.reshape(value_rows.shape[0], -1, 128)
    return jnp.einsum("hqk,khd->qhd", weights, value_heads, preferred_element_type=jnp.float32)


def per_device(
    queries,
    text_cache,
    image_cache,
    fresh_kv,
    fresh_slots,
    fresh_pos,
    image_len,
    stream,
    modulation,
    out_weight,
    up_weight,
    down_weight,
    final_weight,
    latent,
    step_index,
):
    cfg_id = lax.axis_index("cfg")
    req_id = lax.axis_index("req")
    seq_id = lax.axis_index("seq")
    query_rows = queries[0, 0]
    row_count = query_rows.shape[0]
    query_heads = query_rows.reshape(row_count, -1, 128)
    text_kv = text_cache[0, 0]
    image_kv = image_cache[0, 0]
    angles = rope_angles(fresh_pos[:, 0, :])
    fresh_keys = rotate(fresh_kv[0, 0, 0].astype(jnp.float32), angles).astype(jnp.bfloat16)
    fresh_pair = jnp.stack([fresh_keys, fresh_kv[0, 0, 1]], axis=0)
    all_fresh, proj_cols, up_cols, down_rows = (
        lax.all_gather(fresh_pair, "seq", axis=1, tiled=True),
        lax.all_gather(out_weight, "seq", axis=0, tiled=True),
        lax.all_gather(up_weight, "seq", axis=0, tiled=True),
        lax.all_gather(down_weight, "seq", axis=1, tiled=True),
    )
    image_kv = image_kv.at[:, fresh_slots[0], :].set(all_fresh)
    length = lax.dynamic_index_in_dim(image_len, req_id, 0, keepdims=False)
    image_total = image_kv.shape[1]
    text_scores = head_scores(query_heads, text_kv[0])
    text_best = jnp.max(text_scores, axis=-1, keepdims=True)
    live_keys = (jnp.arange(image_total) < length)[None, None, :]
    image_scores = jnp.where(live_keys, head_scores(query_heads, image_kv[0]), -jnp.inf)
    row_max = jnp.maximum(text_best, jnp.max(image_scores, axis=-1, keepdims=True))
    text_probs = jnp.exp(text_scores - row_max)
    image_probs = jnp.exp(image_scores - row_max)
    total = jnp.sum(text_probs, axis=-1) + jnp.sum(image_probs, axis=-1)
    mixed = head_mix(text_probs.astype(jnp.bfloat16), text_kv[1]) + head_mix(
        image_probs.astype(jnp.bfloat16), image_kv[1]
    )
    attended = (
        (mixed / jnp.transpose(total)[:, :, None]).reshape(row_count, -1).astype(jnp.bfloat16)
    )
    projected = jnp.dot(
        lax.all_gather(attended, "req", axis=0, tiled=True),
        proj_cols,
        preferred_element_type=jnp.float32,
    )
    requests = stream.shape[1]
    col_count = stream.shape[3]
    mod_half = lax.dynamic_index_in_dim(modulation, cfg_id, 0, keepdims=False)
    gate_cols = lax.dynamic_slice_in_dim(mod_half[:, 0, :], req_id * col_count, col_count, 1)
    residual = (
        stream[0].astype(jnp.float32)
        + gate_cols[:, None, :] * projected.reshape(requests, row_count, col_count)
    ).astype(jnp.bfloat16)
    full_rows = lax.all_gather(
        residual.reshape(requests * row_count, col_count), "req", axis=1, tiled=True
    )
    wide = full_rows.reshape(requests, row_count, -1).astype(jnp.float32)
    average = jnp.mean(wide, axis=-1, keepdims=True)
    centered = wide - average
    spread = jnp.mean(centered * centered, axis=-1, keepdims=True)
    normed = (
        centered * lax.rsqrt(spread + EPSILON) * (1.0 + mod_half[:, 2][:, None, :])
        + mod_half[:, 1][:, None, :]
    )
    normed = normed.astype(jnp.bfloat16).reshape(requests * row_count, -1)

    def rows_product(left_rows, right):
        return jnp.dot(left_rows, right, preferred_element_type=jnp.float32)

    pre_act = rows_product(normed, up_cols)
    activated = jax.nn.gelu(pre_act, approximate=True).astype(jnp.bfloat16)
    mlp_rows = lax.psum_scatter(
        rows_product(activated, down_rows).astype(jnp.bfloat16),
        "req",
        scatter_dimension=0,
        tiled=True,
    ).astype(jnp.float32)
    own_rows = lax.dynamic_slice_in_dim(full_rows, req_id * row_count, row_count, 0)
    gate_two = lax.dynamic_index_in_dim(mod_half[:, 3, :], req_id, 0, keepdims=False)
    block_out = (own_rows.astype(jnp.float32) + gate_two[None, :] * mlp_rows).astype(jnp.bfloat16)
    velocity = jnp.dot(block_out, final_weight, preferred_element_type=jnp.float32).reshape(
        row_count // 2, -1
    )
    lane_count = velocity.shape[1]
    half_lanes = lane_count // 2
    outgoing = lax.dynamic_slice_in_dim(velocity, (1 - cfg_id) * half_lanes, half_lanes, 1)
    own_part = lax.dynamic_slice_in_dim(velocity, cfg_id * half_lanes, half_lanes, 1)
    partner = swapped(outgoing, "cfg", 0)
    cond_part = jnp.where(cfg_id == 0, own_part, partner)
    uncond_part = jnp.where(cfg_id == 0, partner, own_part)
    guided = uncond_part + GUIDANCE * (cond_part - uncond_part)
    level_now = noise_level(step_index[0])
    level_next = noise_level(step_index[0] + 1)
    token_ids = (
        seq_id * row_count
        + 2 * jnp.arange(row_count // 2, dtype=jnp.int32)[:, None]
        + cfg_id
        + jnp.zeros((1, half_lanes), jnp.int32)
    )
    valid = token_ids < length
    current = latent[0]
    latent_next = jnp.where(valid, current + (level_next - level_now) * guided, current)
    denoised = jnp.where(valid, current - level_now * guided, current)
    return (latent_next[None], denoised[None])


def solution(mesh):
    in_specs = (
        P("cfg", "req", "seq", None),
        P("cfg", "req", None, None, None),
        P("cfg", "req", None, None, None),
        P("cfg", "req", None, "seq", None),
        P("req", None),
        P(None, "req", "seq"),
        P(),
        P("cfg", None, "seq", "req"),
        P(),
        P("seq", "req"),
        P("seq", "req"),
        P("req", "seq"),
        P(),
        P("req", "seq", "cfg"),
        P(),
    )
    out_specs = (P("req", "seq", "cfg"), P("req", "seq", "cfg"))
    return jax.shard_map(
        per_device, mesh=mesh, in_specs=in_specs, out_specs=out_specs, check_vma=False
    )
```

profile of v0, /device:TPU:1, one launch (start us, length us, event | category | flops | bytes accessed | tf_op | source)
XLA Modules:
  0.0 484.3 jit_solution(10954910353682535081)
XLA Ops:
  7.2 0.0 all-gather.6.cloned.1.call-start
  7.3 0.8 convert_bitcast_fusion.2
  8.0 0.1 broadcast_multiply_fusion.2
  8.1 0.1 broadcast_multiply_fusion.1
  8.2 0.1 fusion.54
  8.3 0.1 copy.62
  8.4 0.1 copy.65
  8.5 0.9 fusion.58
  9.4 0.3 copy.64
  9.7 1.0 multiply_subtract_fusion
  10.7 0.4 copy.66
  11.1 0.4 copy.67
  11.5 0.1 pad_maximum_fusion
  11.6 0.4 copy.68
  12.1 0.3 copy.70
  12.4 0.1 pad_maximum_fusion.1
  12.5 20.3 %all_gather.18 = bf16[2,96,1536]{2,0,1:T(2,128)(2,1)S(1)} all-gather(bf16[2,6,1536]{2,0,1:T(2,128)(2,1)S(1)} %pad_maximum_fusion.1), channel_id=1, replica_groups=mesh['cfg'=2,'req'=8,'seq'=16] {'seq'}, dimensions={1}, use_global_device_ids=true | all-gather | bytes 626688 | tf_op jit(solution)/shard_map/all_gather | solution.py:90
  32.8 9.4 %copy.107 = bf16[1,1,2,768,1536]{4,2,3,1,0:T(2,128)(2,1)} copy(bf16[1,1,2,768,1536]{4,3,2,1,0:T(8,128)(2,1)} %param.17) | data formatting | bytes 9437184 | tf_op args[2]
  42.2 11.7 %scatter_fusion = bf16[2,768,1536]{2,0,1:T(2,128)(2,1)} fusion(bf16[2,768,1536]{2,0,1:T(2,128)(2,1)} %bitcast.99, s32[96]{0:T(128)S(1)} %fusion.46, bf16[96,2,1536]{2,1,0:T(2,128)(2,1)S(1)} %bitcast.106), kind=kCustom, calls=%fused_computation | custom fusion | bytes 1769856 | tf_op jit(solution)/shard_map/scatter | solution.py:95
  53.9 10.7 %fusion.55 = (bf16[1,768,1536]{2,0,1:T(2,128)(2,1)}, bf16[1,768,1536]{2,0,1:T(2,128)(2,1)}) fusion(bf16[2,768,1536]{2,0,1:T(2,128)(2,1)} %scatter_fusion), kind=kLoop, calls=%fused_computation.100 | loop fusion | bytes 9437184 | tf_op jit(solution)/shard_map/slice | solution.py:107
  64.6 11.7 %copy.72 = bf16[1,768,1536]{1,2,0:T(8,128)(2,1)} copy(bf16[1,768,1536]{2,0,1:T(2,128)(2,1)} %get-tuple-element.3) | data formatting | bytes 4718592 | tf_op jit(solution)/shard_map/slice | solution.py:101
  76.4 0.6 dynamic_slice.24
  76.9 0.6 iota_compare_fusion
  77.6 0.8 reshape_squeeze.15
  78.4 3.7 fusion.56
  82.2 1.7 copy.87
  83.9 1.5 fusion.59
  85.5 0.2 copy-done.3
  85.7 0.6 bitcast_reduce_fusion
  86.3 1.3 copy-done.4
  87.6 1.2 fusion.15
  88.7 1.0 fusion.28
  89.7 1.7 copy.90
  91.4 1.5 convolution_bitcast_fusion.1
  92.9 11.8 %copy.77 = bf16[1,768,1536]{1,2,0:T(8,128)(2,1)} copy(bf16[1,768,1536]{2,0,1:T(2,128)(2,1)} %get-tuple-element.2) | data formatting | bytes 4718592 | tf_op jit(solution)/shard_map/slice | solution.py:107
  104.8 2.7 fusion.27
  107.5 0.7 copy.108
  108.2 0.0 all-gather.8.cloned.1.call-start
  108.2 0.7 all-gather.8.cloned.1.call-update
  108.9 0.3 all-gather.10.cloned.1.call-start
  109.3 0.9 fusion.57
  110.2 39.1 %all-gather.6.cloned.1.call-done = bf16[384,1536]{1,0:T(8,128)(2,1)} async-done(((bf16[48,1536]{1,0:T(8,128)(2,1)}), bf16[384,1536]{1,0:T(8,128)(2,1)}) %all-gather.6.cloned.1.call-update) | async-done | bytes 1179664 | tf_op jit(solution)/shard_map/all_gather | solution.py:113
  149.3 52.0 %all-gather.8.cloned.1.call-done = bf16[1536,384]{1,0:T(8,128)(2,1)} async-done(((bf16[96,384]{1,0:T(8,128)(2,1)}), bf16[1536,384]{1,0:T(8,128)(2,1)}) %all-gather.8.cloned.1.call-update) | async-done | bytes 1179664 | tf_op jit(solution)/shard_map/all_gather | solution.py:91
  201.4 3.1 fusion.18
  204.6 0.0 all-gather.12.cloned.1.call-start
  204.6 0.5 all-gather.12.cloned.1.call-update
  205.2 0.5 all-gather.14.cloned.1.call-update
  205.7 0.0 reduce-scatter.2.cloned.1.call-start
  205.8 38.7 %all-gather.10.cloned.1.call-done = bf16[384,3072]{1,0:T(8,128)(2,1)} async-done(((bf16[384,384]{1,0:T(8,128)(2,1)}), bf16[384,3072]{1,0:T(8,128)(2,1)}) %all-gather.10.cloned.1.call-update) | async-done | bytes 2359312 | tf_op jit(solution)/shard_map/all_gather | solution.py:125
  244.5 2.2 convert_reduce_fusion
  246.7 0.2 copy-done.2
  246.9 0.8 fusion.2
  247.6 2.6 fusion.5
  250.3 78.9 %all-gather.12.cloned.1.call-done = bf16[3072,1536]{1,0:T(8,128)(2,1)} async-done(((bf16[192,1536]{1,0:T(8,128)(2,1)}), bf16[3072,1536]{1,0:T(8,128)(2,1)}) %all-gather.12.cloned.1.call-update) | async-done | bytes 9437200 | tf_op jit(solution)/shard_map/all_gather | solution.py:92
  329.2 82.8 %all-gather.14.cloned.1.call-done = bf16[1536,3072]{0,1:T(8,128)(2,1)} async-done(((bf16[1536,192]{0,1:T(8,128)(2,1)}), bf16[1536,3072]{0,1:T(8,128)(2,1)}) %all-gather.14.cloned.1.call-update) | async-done | bytes 9437200 | tf_op jit(solution)/shard_map/all_gather | solution.py:93
  412.0 16.2 %convolution_convert_fusion = bf16[384,3072]{1,0:T(8,128)(2,1)} fusion(bf16[1536,3072]{0,1:T(8,128)(2,1)} %all-gather.14.cloned.1.call-done, bf16[384,3072]{1,0:T(8,128)(2,1)} %fusion.5, bf16[3072,1536]{1,0:T(8,128)(2,1)} %all-gather.12.cloned.1.call-done), kind=kOutput, calls=%fused_computation.10 | convolution fusion | flops 7254245376 | bytes 23592960 | tf_op jit(solution)/shard_map/dot_general | solution.py:139
  428.1 0.8 constant_dynamic-slice_fusion.1
  428.9 37.9 %reduce-scatter.2.cloned.1.call-done = bf16[48,3072]{1,0:T(8,128)(2,1)} async-done(((bf16[384,3072]{1,0:T(8,128)(2,1)}), bf16[48,3072]{1,0:T(8,128)(2,1)}) %reduce-scatter.2.cloned.1.call-update) | async-done | bytes 294928 | tf_op jit(solution)/shard_map/reduce_scatter | solution.py:143
  466.8 1.8 fusion.37
  468.6 0.8 reshape.245
  469.4 0.1 constant_dynamic-slice_fusion
  469.5 5.2 %collective-permute-start = (f32[24,64]{1,0:T(8,128)S(1)}, f32[24,64]{1,0:T(8,128)S(1)}, u32[]{:S(2)}, u32[]{:S(2)}) collective-permute-start(f32[24,64]{1,0:T(8,128)S(1)} %constant_dynamic-slice_fusion), channel_id=1, source_target_pairs={{0,128},{128,0},{1,129},{129,1},{2,130},{130,2},{3,131},{131,3},{4... | collective-permute-start | bytes 18440 | tf_op jit(solution)/shard_map/ppermute | solution.py:21
  474.7 0.6 add_compare_fusion
  476.0 1.4 fusion.44
  (49 shorter events, 0.4 us)
Async XLA Ops:
  7.2 102.0 %copy-start = (f32[2,8,4,3072]{3,2,1,0:T(4,128)S(1)}, f32[2,8,4,3072]{3,2,1,0:T(4,128)}, u32[]{:S(2)}) copy-start(f32[2,8,4,3072]{3,2,1,0:T(4,128)} %param.23) | copy-start | bytes 2359300
  7.2 142.1 %all-gather.6.cloned.1.call-start = ((), (), s32[]{:S(2)}) async-start(), calls=%async_computation.1 | async-start | bytes 1327104 | tf_op jit(solution)/shard_map/all_gather | solution.py:113
  32.8 9.4 %copy-start.14 = (s32[1,96]{1,0:T(1,128)S(1)}, s32[1,96]{1,0:T(1,128)}, u32[]{:S(2)}) copy-start(s32[1,96]{1,0:T(1,128)} %param.19) | copy-start | bytes 1156
  64.6 11.8 %copy-start.15 = (s32[8]{0:T(128)S(1)}, s32[8]{0:T(128)}, u32[]{:S(2)}) copy-start(s32[8]{0:T(128)} %param.21) | copy-start | bytes 100
  64.6 13.0 %copy-start.10 = (bf16[1,1,48,1536]{3,2,1,0:T(8,128)(2,1)S(1)}, bf16[1,1,48,1536]{3,2,1,0:T(8,128)(2,1)}, u32[]{:S(2)}) copy-start(bf16[1,1,48,1536]{3,2,1,0:T(8,128)(2,1)} %param.15) | copy-start | bytes 442372
  77.6 7.9 %copy-start.12 = (pred[768]{0:T(1024)(128)(4,1)}, pred[768]{0:T(1024)(128)(4,1)S(1)}, u32[]{:S(2)}) copy-start(pred[768]{0:T(1024)(128)(4,1)S(1)} %iota_compare_fusion) | copy-start | bytes 2308
  83.9 1.8 copy-start.3
  83.9 1.8 copy-start.6
  86.3 1.3 copy-start.4
  92.9 11.9 %copy-start.11 = (f32[12,48]{1,0:T(8,128)S(1)}, f32[12,48]{1,0:T(8,128)}, u32[]{:S(2)}) copy-start(f32[12,48]{1,0:T(8,128)} %fusion.28) | copy-start | bytes 6916
  92.9 11.9 %copy-start.5 = (f32[12,768,48]{1,2,0:T(8,128)S(1)}, f32[12,768,48]{1,2,0:T(8,128)}, u32[]{:S(2)}) copy-start(f32[12,768,48]{1,2,0:T(8,128)} %copy-done.4) | copy-start | bytes 5308420
  92.9 11.9 %copy-start.9 = (f32[48,12,128]{2,0,1:T(8,128)S(1)}, f32[48,12,128]{2,0,1:T(8,128)}, u32[]{:S(2)}) copy-start(f32[48,12,128]{2,0,1:T(8,128)} %convolution_bitcast_fusion.1) | copy-start | bytes 884740
  92.9 11.9 %copy-start.13 = (pred[768]{0:T(1024)(128)(4,1)S(1)}, pred[768]{0:T(1024)(128)(4,1)}, u32[]{:S(2)}) copy-start(pred[768]{0:T(1024)(128)(4,1)} %copy-done.12) | copy-start | bytes 2308
  107.5 93.9 %copy-start.8 = (bf16[1,8,48,384]{3,2,1,0:T(8,128)(2,1)S(1)}, bf16[1,8,48,384]{3,2,1,0:T(8,128)(2,1)}, u32[]{:S(2)}) copy-start(bf16[1,8,48,384]{3,2,1,0:T(8,128)(2,1)} %param.22) | copy-start | bytes 884740
  108.2 93.2 %all-gather.8.cloned.1.call-start = ((), (), s32[]{:S(2)}) async-start(), calls=%async_computation.2 | async-start | bytes 1253376 | tf_op jit(solution)/shard_map/all_gather | solution.py:91
  108.9 135.6 %all-gather.10.cloned.1.call-start = ((), (), s32[]{:S(2)}) async-start(), calls=%async_computation.3 | async-start | bytes 2654208 | tf_op jit(solution)/shard_map/all_gather | solution.py:125
  204.6 124.6 %all-gather.12.cloned.1.call-start = ((), (), s32[]{:S(2)}) async-start(), calls=%async_computation.4 | async-start | bytes 10027008 | tf_op jit(solution)/shard_map/all_gather | solution.py:92
  205.1 206.8 %all-gather.14.cloned.1.call-start = ((), (), s32[]{:S(2)}) async-start(), calls=%async_computation.5 | async-start | bytes 10027008 | tf_op jit(solution)/shard_map/all_gather | solution.py:93
  205.7 261.1 %reduce-scatter.2.cloned.1.call-start = ((), (), s32[]{:S(2)}) async-start(), calls=%async_computation.6 | async-start | bytes 2654208 | tf_op jit(solution)/shard_map/reduce_scatter | solution.py:143
  244.5 2.4 copy-start.2
  412.0 65.5 %copy-start.1 = (f32[2,8,4,3072]{3,2,1,0:T(4,128)S(1)}, f32[2,8,4,3072]{3,2,1,0:T(4,128)}, u32[]{:S(2)}) copy-start(f32[2,8,4,3072]{3,2,1,0:T(4,128)} %param.23) | copy-start | bytes 2359300
  428.1 38.7 %copy-start.7 = (bf16[3072,64]{0,1:T(8,128)(2,1)S(1)}, bf16[3072,64]{0,1:T(8,128)(2,1)}, u32[]{:S(2)}) copy-start(bf16[3072,64]{0,1:T(8,128)(2,1)} %param.27) | copy-start | bytes 1179652
  469.5 6.5 %collective-permute-start = (f32[24,64]{1,0:T(8,128)S(1)}, f32[24,64]{1,0:T(8,128)S(1)}, u32[]{:S(2)}, u32[]{:S(2)}) collective-permute-start(f32[24,64]{1,0:T(8,128)S(1)} %constant_dynamic-slice_fusion), channel_id=1, source_target_pairs={{0,128},{128,0},{1,129},{129,1},{2,130},{130,2},{3,131},{131,3},{4... | collective-permute-start | bytes 18440 | tf_op jit(solution)/shard_map/ppermute | solution.py:21
Sparse Core Ops, SparseCore 0:
  108.3 40.9 all-gather.5
  151.8 49.5 all-gather.7
  204.7 39.7 all-gather.9
  246.8 82.3 all-gather.11
  331.5 80.4 all-gather.13
  428.3 38.5 reduce-scatter.1
where the time goes:
time: 486 us; the launch traced here: 484 us
  waiting for transfers between devices  331 us (68%)
  local copies, waits for them, and re-layouts  71.1 us (15%)
  matrix products  27.3 us (6%)
  blocking collectives  20.3 us (4%)
  between operations  15.2 us (3%)
  other arithmetic  13.6 us (3%)
  starting transfers between devices  5.61 us (1%)
    all_gather x1, waiting for transfers between devices, per_device(): lax.all_gather(down_weight, 'seq', axis=1, tiled=True)  82.8 us
    all_gather x1, waiting for transfers between devices, per_device(): lax.all_gather(up_weight, 'seq', axis=0, tiled=True)  78.9 us
    all_gather x1, waiting for transfers between devices, per_device(): lax.all_gather(out_weight, 'seq', axis=0, tiled=True)  52 us
    all_gather x1, waiting for transfers between devices, per_device(): lax.all_gather(attended, 'req', axis=0, tiled=True)  39.1 us
    all_gather x1, waiting for transfers between devices, per_device(): lax.all_gather(residual.reshape(requests * row_count, col_count), 'req',...  38.7 us
    reduce_scatter x1, waiting for transfers between devices, per_device(): lax.psum_scatter(rows_product(activated, down_rows).astype(jnp.bfloat16),...  37.9 us
    slice x2, local copies, waits for them, and re-layouts, per_device(): image_kv[1]  22.5 us
    all_gather x1, blocking collectives, per_device(): lax.all_gather(fresh_pair, 'seq', axis=1, tiled=True)  20.3 us
  transfers between devices with their start and end apart: 7, of which 6 were waited for; matrix products, arithmetic and copies ran while one was open for 2% of the time, Pallas kernels for 0%

commit v1 on v0

--- a/solution.py
+++ b/solution.py
@@ -122,9 +122,9 @@
         stream[0].astype(jnp.float32)
         + gate_cols[:, None, :] * projected.reshape(requests, row_count, col_count)
     ).astype(jnp.bfloat16)
-    full_rows = lax.all_gather(
-        residual.reshape(requests * row_count, col_count), "req", axis=1, tiled=True
-    )
+    part = residual.reshape(requests * row_count, col_count)
+    sent = jnp.stack([part] * lax.axis_size("req"))
+    full_rows = jnp.concatenate(lax.all_to_all(sent, "req", 0, 0), axis=1)
     wide = full_rows.reshape(requests, row_count, -1).astype(jnp.float32)
     average = jnp.mean(wide, axis=-1, keepdims=True)
     centered = wide - average

time: 486 us -> 442 us (0.909)
  waiting for transfers between devices: 331 us -> 263 us
  local copies, waits for them, and re-layouts: 71.1 us -> 92.8 us
  starting transfers between devices: 5.61 us -> 11.9 us
    all_gather x1, waiting for transfers between devices: 82.8 us -> 14 us  [per_device(): lax.all_gather(down_weight, 'seq', axis=1, tiled=True)]
    all_to_all x0 -> x1, waiting for transfers between devices: none -> 39.5 us  [per_device(): full_rows = jnp.concatenate(lax.all_to_all(sent, 'req', 0, 0), axis=1)]
    all_gather x1 -> x0, waiting for transfers between devices: 38.7 us -> none  [per_device(): lax.all_gather(residual.reshape(requests * row_count, col_count), 'req',...]
    mul x0 -> x2, local copies, waits for them, and re-layouts: none -> 8.99 us  [per_device(): centered * lax.rsqrt(spread + EPSILON) * (1.0 + mod_half[:, 2][:, None, :])]
    add x0 -> x2, local copies, waits for them, and re-layouts: none -> 8.77 us  [per_device(): centered * lax.rsqrt(spread + EPSILON) * (1.0 + mod_half[:, 2][:, None, :])]
    all_to_all x0 -> x1, starting transfers between devices: none -> 6.73 us  [per_device(): full_rows = jnp.concatenate(lax.all_to_all(sent, 'req', 0, 0), axis=1)]
    unnamed x38 -> x35, local copies, waits for them, and re-layouts: 14.6 us -> 15.8 us
  transfers between devices with their start and end apart: 7 -> 7, of which waited for: 6 -> 6; matrix products, arithmetic and copies ran while one was open for 2% -> 6% of each run, Pallas kernels for 0% -> 0%
where the time goes in v1:
time: 442 us; the launch traced here: 441 us
  waiting for transfers between devices  263 us (60%)
  local copies, waits for them, and re-layouts  92.8 us (21%)
  matrix products  28.5 us (6%)
  blocking collectives  20.3 us (5%)
  between operations  14.9 us (3%)
  starting transfers between devices  11.9 us (3%)
  other arithmetic  9.04 us (2%)
    all_gather x1, waiting for transfers between devices, per_device(): lax.all_gather(up_weight, 'seq', axis=0, tiled=True)  82.8 us
    all_gather x1, waiting for transfers between devices, per_device(): lax.all_gather(out_weight, 'seq', axis=0, tiled=True)  52 us
    all_to_all x1, waiting for transfers between devices, per_device(): full_rows = jnp.concatenate(lax.all_to_all(sent, 'req', 0, 0), axis=1)  39.5 us
    all_gather x1, waiting for transfers between devices, per_device(): lax.all_gather(attended, 'req', axis=0, tiled=True)  38.1 us
    reduce_scatter x1, waiting for transfers between devices, per_device(): lax.psum_scatter(rows_product(activated, down_rows).astype(jnp.bfloat16),...  35.3 us
    slice x2, local copies, waits for them, and re-layouts, per_device(): image_kv[1]  22.5 us
    all_gather x1, blocking collectives, per_device(): lax.all_gather(fresh_pair, 'seq', axis=1, tiled=True)  20.3 us
    dot_general x1, matrix products, rows_product(): return jnp.dot(left_rows, right, preferred_element_type=jnp.float32)  18.7 us
  transfers between devices with their start and end apart: 7, of which 6 were waited for; matrix products, arithmetic and copies ran while one was open for 6% of the time, Pallas kernels for 0%

profile of v1, /device:TPU:1, one launch (start us, length us, event | category | flops | bytes accessed | tf_op | source)
XLA Modules:
  0.0 440.8 jit_solution(15359245102516222647)
XLA Ops:
  7.3 0.8 convert_bitcast_fusion.2
  8.2 0.1 fusion.43
  8.3 0.1 copy.90
  8.4 0.1 copy.93
  8.5 0.9 fusion.47
  9.4 0.3 copy.92
  9.7 1.0 multiply_subtract_fusion
  10.7 0.4 copy.94
  11.1 0.4 copy.95
  11.5 0.1 pad_maximum_fusion
  11.6 0.4 copy.96
  12.1 0.3 copy.98
  12.4 0.1 pad_maximum_fusion.1
  12.5 20.3 %all_gather.15 = bf16[2,96,1536]{2,0,1:T(2,128)(2,1)S(1)} all-gather(bf16[2,6,1536]{2,0,1:T(2,128)(2,1)S(1)} %pad_maximum_fusion.1), channel_id=1, replica_groups=mesh['cfg'=2,'req'=8,'seq'=16] {'seq'}, dimensions={1}, use_global_device_ids=true | all-gather | bytes 626688 | tf_op jit(solution)/shard_map/all_gather | solution.py:90
  32.8 9.4 %copy.135 = bf16[1,1,2,768,1536]{4,2,3,1,0:T(2,128)(2,1)} copy(bf16[1,1,2,768,1536]{4,3,2,1,0:T(8,128)(2,1)} %param.17) | data formatting | bytes 9437184 | tf_op args[2]
  42.3 11.7 %scatter_fusion = bf16[2,768,1536]{2,0,1:T(2,128)(2,1)} fusion(bf16[2,768,1536]{2,0,1:T(2,128)(2,1)} %bitcast.98, s32[96]{0:T(128)S(1)} %fusion.39, bf16[96,2,1536]{2,1,0:T(2,128)(2,1)S(1)} %bitcast.109), kind=kCustom, calls=%fused_computation | custom fusion | bytes 1769856 | tf_op jit(solution)/shard_map/scatter | solution.py:95
  53.9 10.7 %fusion.44 = (bf16[1,768,1536]{2,0,1:T(2,128)(2,1)}, bf16[1,768,1536]{2,0,1:T(2,128)(2,1)}) fusion(bf16[2,768,1536]{2,0,1:T(2,128)(2,1)} %scatter_fusion), kind=kLoop, calls=%fused_computation.91 | loop fusion | bytes 9437184 | tf_op jit(solution)/shard_map/slice | solution.py:107
  64.6 11.7 %copy.100 = bf16[1,768,1536]{1,2,0:T(8,128)(2,1)} copy(bf16[1,768,1536]{2,0,1:T(2,128)(2,1)} %get-tuple-element.3) | data formatting | bytes 4718592 | tf_op jit(solution)/shard_map/slice | solution.py:101
  76.4 0.7 dynamic_slice.24
  77.0 0.7 iota_compare_fusion
  77.8 0.8 reshape_squeeze.15
  78.6 3.7 fusion.45
  82.3 1.7 copy.116
  84.1 1.5 fusion.48
  85.6 0.2 copy-done.2
  85.8 0.6 bitcast_reduce_fusion
  86.4 1.3 copy-done.3
  87.7 1.2 fusion.14
  88.9 1.0 fusion.22
  89.9 1.7 copy.119
  91.6 1.4 convolution_bitcast_fusion.1
  93.0 11.8 %copy.105 = bf16[1,768,1536]{1,2,0:T(8,128)(2,1)} copy(bf16[1,768,1536]{2,0,1:T(2,128)(2,1)} %get-tuple-element.2) | data formatting | bytes 4718592 | tf_op jit(solution)/shard_map/slice | solution.py:107
  104.9 2.7 fusion.21
  107.6 0.7 copy.137
  108.3 0.7 all-gather.7.cloned.1.call-update
  109.1 0.7 all-gather.11.cloned.1.call-update
  109.8 0.3 all-gather.9.cloned.1.call-start
  110.0 0.3 all-gather.9.cloned.1.call-update
  110.4 0.2 copy.136
  110.6 0.7 fusion.46
  111.3 38.1 %all-gather.5.cloned.1.call-done = bf16[384,1536]{1,0:T(8,128)(2,1)} async-done(((bf16[48,1536]{1,0:T(8,128)(2,1)}), bf16[384,1536]{1,0:T(8,128)(2,1)}) %all-gather.5.cloned.1.call-update) | async-done | bytes 1179664 | tf_op jit(solution)/shard_map/all_gather | solution.py:113
  149.4 52.0 %all-gather.7.cloned.1.call-done = bf16[1536,384]{1,0:T(8,128)(2,1)} async-done(((bf16[96,384]{1,0:T(8,128)(2,1)}), bf16[1536,384]{1,0:T(8,128)(2,1)}) %all-gather.7.cloned.1.call-update) | async-done | bytes 1179664 | tf_op jit(solution)/shard_map/all_gather | solution.py:91
  201.5 2.4 fusion.17
  203.9 0.2 copy.108
  204.1 1.6 stack.15
  205.7 6.7 %all-to-all-start = ((bf16[8,384,384]{1,2,0:T(8,128)(2,1)}), bf16[8,384,384]{1,2,0:T(8,128)(2,1)S(1)}, u32[]{:S(2)}, u32[]{:S(2)}) async-start(bf16[8,384,384]{1,2,0:T(8,128)(2,1)} %stack.15), calls=%async_computation | async-start | bytes 4718592 | tf_op jit(solution)/shard_map/all_to_all | solution.py:127
  212.5 2.8 mul.272
  215.3 6.2 %copy.110 = f32[384,3072]{0,1:T(8,128)} copy(f32[384,3072]{1,0:T(8,128)} %bitcast.101) | data formatting | bytes 9437184 | tf_op jit(solution)/shard_map/mul | solution.py:133
  221.5 2.7 add.165
  224.2 6.1 %copy.111 = f32[384,3072]{0,1:T(8,128)} copy(f32[384,3072]{1,0:T(8,128)} %bitcast.102) | data formatting | bytes 9437184 | tf_op jit(solution)/shard_map/add | solution.py:133
  230.3 39.5 %all-to-all-done = bf16[8,384,384]{1,2,0:T(8,128)(2,1)S(1)} async-done(((bf16[8,384,384]{1,2,0:T(8,128)(2,1)}), bf16[8,384,384]{1,2,0:T(8,128)(2,1)S(1)}, u32[]{:S(2)}, u32[]{:S(2)}) %all-to-all-start) | async-done | bytes 2359328 | tf_op jit(solution)/shard_map/all_to_all | solution.py:127
  269.7 0.4 convert_reduce_fusion
  270.2 0.7 fusion.1
  270.9 14.0 %all-gather.11.cloned.1.call-done = bf16[1536,3072]{0,1:T(8,128)(2,1)} async-done(((bf16[1536,192]{0,1:T(8,128)(2,1)}), bf16[1536,3072]{0,1:T(8,128)(2,1)}) %all-gather.11.cloned.1.call-update) | async-done | bytes 9437200 | tf_op jit(solution)/shard_map/all_gather | solution.py:93
  284.9 82.8 %all-gather.9.cloned.1.call-done = bf16[3072,1536]{1,0:T(8,128)(2,1)} async-done(((bf16[192,1536]{1,0:T(8,128)(2,1)}), bf16[3072,1536]{1,0:T(8,128)(2,1)}) %all-gather.9.cloned.1.call-update) | async-done | bytes 9437200 | tf_op jit(solution)/shard_map/all_gather | solution.py:92
  367.7 18.7 %convolution_convert_fusion = bf16[384,3072]{1,0:T(8,128)(2,1)} fusion(bf16[1536,3072]{0,1:T(8,128)(2,1)} %all-gather.11.cloned.1.call-done, bf16[3072,1536]{1,0:T(8,128)(2,1)} %all-gather.9.cloned.1.call-done, f32[384,3072]{0,1:T(8,128)} %copy.111, f32[384,3072]{0,1:T(8,128)} %copy.110, bf16[384,3072]{0,1:T(8,128)(2,1)S(1)} %bitcast.99, ...), kind=kOutput, calls=%fused_computation.7 | convolution fusion | flops 7261323264 | bytes 33033216 | tf_op jit(solution)/shard_map/dot_general | solution.py:139
  386.4 1.0 constant_dynamic-slice_fusion.1
  387.4 1.2 constant_dynamic-slice_fusion.2
  388.6 1.4 copy.120
  390.0 35.3 %reduce-scatter.2.cloned.1.call-done = bf16[48,3072]{1,0:T(8,128)(2,1)} async-done(((bf16[384,3072]{1,0:T(8,128)(2,1)}), bf16[48,3072]{1,0:T(8,128)(2,1)}) %reduce-scatter.2.cloned.1.call-update) | async-done | bytes 294928 | tf_op jit(solution)/shard_map/reduce_scatter | solution.py:143
  425.3 1.2 fusion.31
  426.6 4.8 %collective-permute-start = (f32[24,64]{1,0:T(8,128)S(1)}, f32[24,64]{1,0:T(8,128)S(1)}, u32[]{:S(2)}, u32[]{:S(2)}) collective-permute-start(f32[24,64]{1,0:T(8,128)S(1)} %constant_dynamic-slice_fusion), channel_id=1, source_target_pairs={{0,128},{128,0},{1,129},{129,1},{2,130},{130,2},{3,131},{131,3},{4... | collective-permute-start | bytes 18440 | tf_op jit(solution)/shard_map/ppermute | solution.py:21
  431.4 0.7 add_compare_fusion
  432.9 1.4 fusion.38
  (52 shorter events, 0.7 us)
Async XLA Ops:
  7.2 103.2 %copy-start = (f32[2,8,4,3072]{3,2,1,0:T(4,128)S(1)}, f32[2,8,4,3072]{3,2,1,0:T(4,128)}, u32[]{:S(2)}) copy-start(f32[2,8,4,3072]{3,2,1,0:T(4,128)} %param.23) | copy-start | bytes 2359300
  7.2 142.2 %all-gather.5.cloned.1.call-start = ((), (), s32[]{:S(2)}) async-start(), calls=%async_computation.2 | async-start | bytes 1327104 | tf_op jit(solution)/shard_map/all_gather | solution.py:113
  32.8 9.4 %copy-start.13 = (s32[1,96]{1,0:T(1,128)S(1)}, s32[1,96]{1,0:T(1,128)}, u32[]{:S(2)}) copy-start(s32[1,96]{1,0:T(1,128)} %param.19) | copy-start | bytes 1156
  64.6 11.8 %copy-start.14 = (s32[8]{0:T(128)S(1)}, s32[8]{0:T(128)}, u32[]{:S(2)}) copy-start(s32[8]{0:T(128)} %param.21) | copy-start | bytes 100
  64.6 13.1 %copy-start.9 = (bf16[1,1,48,1536]{3,2,1,0:T(8,128)(2,1)S(1)}, bf16[1,1,48,1536]{3,2,1,0:T(8,128)(2,1)}, u32[]{:S(2)}) copy-start(bf16[1,1,48,1536]{3,2,1,0:T(8,128)(2,1)} %param.15) | copy-start | bytes 442372
  77.7 7.8 %copy-start.11 = (pred[768]{0:T(1024)(128)(4,1)}, pred[768]{0:T(1024)(128)(4,1)S(1)}, u32[]{:S(2)}) copy-start(pred[768]{0:T(1024)(128)(4,1)S(1)} %iota_compare_fusion) | copy-start | bytes 2308
  84.0 1.8 copy-start.2
  84.0 1.8 copy-start.5
  86.4 1.3 copy-start.3
  93.0 11.8 %copy-start.10 = (f32[12,48]{1,0:T(8,128)S(1)}, f32[12,48]{1,0:T(8,128)}, u32[]{:S(2)}) copy-start(f32[12,48]{1,0:T(8,128)} %fusion.22) | copy-start | bytes 6916
  93.0 11.8 %copy-start.4 = (f32[12,768,48]{1,2,0:T(8,128)S(1)}, f32[12,768,48]{1,2,0:T(8,128)}, u32[]{:S(2)}) copy-start(f32[12,768,48]{1,2,0:T(8,128)} %copy-done.3) | copy-start | bytes 5308420
  93.0 11.8 %copy-start.8 = (f32[48,12,128]{2,0,1:T(8,128)S(1)}, f32[48,12,128]{2,0,1:T(8,128)}, u32[]{:S(2)}) copy-start(f32[48,12,128]{2,0,1:T(8,128)} %convolution_bitcast_fusion.1) | copy-start | bytes 884740
  93.0 11.8 %copy-start.12 = (pred[768]{0:T(1024)(128)(4,1)S(1)}, pred[768]{0:T(1024)(128)(4,1)}, u32[]{:S(2)}) copy-start(pred[768]{0:T(1024)(128)(4,1)} %copy-done.11) | copy-start | bytes 2308
  107.6 93.9 %copy-start.7 = (bf16[1,8,48,384]{3,2,1,0:T(8,128)(2,1)S(1)}, bf16[1,8,48,384]{3,2,1,0:T(8,128)(2,1)}, u32[]{:S(2)}) copy-start(bf16[1,8,48,384]{3,2,1,0:T(8,128)(2,1)} %param.22) | copy-start | bytes 884740
  108.3 93.2 %all-gather.7.cloned.1.call-start = ((), (), s32[]{:S(2)}) async-start(), calls=%async_computation.3 | async-start | bytes 1253376 | tf_op jit(solution)/shard_map/all_gather | solution.py:91
  109.0 175.9 %all-gather.11.cloned.1.call-start = ((), (), s32[]{:S(2)}) async-start(), calls=%async_computation.5 | async-start | bytes 10027008 | tf_op jit(solution)/shard_map/all_gather | solution.py:93
  109.8 257.9 %all-gather.9.cloned.1.call-start = ((), (), s32[]{:S(2)}) async-start(), calls=%async_computation.4 | async-start | bytes 10027008 | tf_op jit(solution)/shard_map/all_gather | solution.py:92
  205.7 64.0 %all-to-all-start = ((bf16[8,384,384]{1,2,0:T(8,128)(2,1)}), bf16[8,384,384]{1,2,0:T(8,128)(2,1)S(1)}, u32[]{:S(2)}, u32[]{:S(2)}) async-start(bf16[8,384,384]{1,2,0:T(8,128)(2,1)} %stack.15), calls=%async_computation | async-start | bytes 4718592 | tf_op jit(solution)/shard_map/all_to_all | solution.py:127
  212.5 212.8 %reduce-scatter.2.cloned.1.call-start = ((), (), s32[]{:S(2)}) async-start(), calls=%async_computation.6 | async-start | bytes 2654208 | tf_op jit(solution)/shard_map/reduce_scatter | solution.py:143
  386.4 38.9 %copy-start.6 = (bf16[3072,64]{0,1:T(8,128)(2,1)S(1)}, bf16[3072,64]{0,1:T(8,128)(2,1)}, u32[]{:S(2)}) copy-start(bf16[3072,64]{0,1:T(8,128)(2,1)} %param.27) | copy-start | bytes 1179652
  386.4 47.9 %copy-start.1 = (f32[2,8,4,3072]{3,2,1,0:T(4,128)S(1)}, f32[2,8,4,3072]{3,2,1,0:T(4,128)}, u32[]{:S(2)}) copy-start(f32[2,8,4,3072]{3,2,1,0:T(4,128)} %param.23) | copy-start | bytes 2359300
  426.6 6.2 %collective-permute-start = (f32[24,64]{1,0:T(8,128)S(1)}, f32[24,64]{1,0:T(8,128)S(1)}, u32[]{:S(2)}, u32[]{:S(2)}) collective-permute-start(f32[24,64]{1,0:T(8,128)S(1)} %constant_dynamic-slice_fusion), channel_id=1, source_target_pairs={{0,128},{128,0},{1,129},{129,1},{2,130},{130,2},{3,131},{131,3},{4... | collective-permute-start | bytes 18440 | tf_op jit(solution)/shard_map/ppermute | solution.py:21
Sparse Core Ops, SparseCore 0:
  108.4 40.9 all-gather.4
  151.8 49.5 all-gather.6
  203.9 80.9 all-gather.10
  287.2 80.4 all-gather.8
  386.5 38.7 reduce-scatter.1
